TPU v7x, 32 devices: a whole 2x2x4 slice. The times are simulated.
32 devices in a mesh: dp: 4 (over z), row: 2 (over core), col: 4 (over y, x).
Axes of the slice: x: 2, y: 2, z: 4, core: 2. Of those that a mesh axis runs over, the one named last changes fastest.
Arguments:
- tokens: float32 [1024, 1024], P(('dp', 'row'), 'col'), may hold values from -6 to 6
- segment_ids: int32 [1024], P('dp'), may hold values from 0 to 1023, as said below
- norm_gain: float32 [1024], P('col'), may hold values from 0.5 to 1.5
- in_weight: bfloat16 [1024, 3, 1024], P('col', None, 'row'), may hold values from -0.1875 to 0.1875
- conv_taps: float32 [3, 1024], P(None, ('row', 'col')), may hold values from -3 to 3
- out_weight: bfloat16 [1024, 1024], P('row', 'col'), may hold values from -0.1875 to 0.1875
- ffn_gain: float32 [1024], P('col'), may hold values from 0.5 to 1.5
- gate_weight: bfloat16 [1024, 4608], P('col', 'row'), may hold values from -0.1875 to 0.1875
- up_weight: bfloat16 [1024, 4608], P('col', 'row'), may hold values from -0.1875 to 0.1875
- down_weight: bfloat16 [4608, 1024], P('row', 'col'), may hold values from -0.09375 to 0.09375
- out_grad: float32 [1024, 1024], P(('dp', 'row'), 'col'), may hold values from -6 to 6
Outputs:
- block_out: float32 [1024, 1024], P(('dp', 'row'), 'col')
- in_grad: float32 [1024, 1024], P(('dp', 'row'), 'col')
- grad_norm_gain: float32 [1024], P('col')
- grad_in_weight: float32 [1024, 3, 1024], P('col', None, 'row')
- grad_conv_taps: float32 [3, 1024], P(None, ('row', 'col'))
- grad_out_weight: float32 [1024, 1024], P('row', 'col')
- grad_ffn_gain: float32 [1024], P('col')
- grad_gate_weight: float32 [1024, 4608], P('col', 'row')
- grad_up_weight: float32 [1024, 4608], P('col', 'row')
- grad_down_weight: float32 [4608, 1024], P('row', 'col')
Inputs may be any that keep to these rules, and one draw needn't show every extreme that they name: `segment_ids`: ids never fall along the tokens; every aligned sequence of 256 consecutive tokens starts a new id and changes id again at least once inside; runs of one id have 200 to 2000 tokens except where a sequence's start or end cuts them; the last token's id is 1023.
All inputs are finite; a program needn't handle non-finite values.
Results may differ from a plain program's by a relative error of at most 0.0094.
Values may be sent and summed in bfloat16 or wider, within the bound.
No kernel may reach another device: no remote copies, remote signals or barrier semaphores. Data moves between devices by JAX's collectives and lax.ppermute only.
A program may use at most 128 MiB of HBM per device.

v0:
```python
import jax
import jax.numpy as jnp
from jax import lax
from jax.sharding import PartitionSpec as P

D = 1024
epsilon = 1e-05


def shifted(source, amount):
    filler = jnp.zeros((amount,) + source.shape[1:], source.dtype)
    return jnp.concatenate([filler, source[:-amount]], axis=0)


def lifted(source, amount):
    filler = jnp.zeros((amount,) + source.shape[1:], source.dtype)
    return jnp.concatenate([source[amount:], filler], axis=0)


def dot_rows(left, right):
    return lax.dot_general(
        left, right, (((0,), (0,)), ((), ())), preferred_element_type=jnp.float32
    )


def dot_cols(left, right):
    return lax.dot_general(
        left, right, (((1,), (1,)), ((), ())), preferred_element_type=jnp.float32
    )


def sum_rows(entries):
    return lax.psum(jnp.sum(entries, axis=1, keepdims=True), "col")


def gather_rows(shard_part):
    return lax.all_gather(shard_part, "row", axis=0, tiled=True)


def reduce_cols(partial_value):
    return lax.psum_scatter(partial_value, "col", scatter_dimension=2, tiled=True)


def share_cols(shard_part):
    return lax.all_gather(shard_part, "col", axis=2, tiled=True)


def reduce_rows(term, local_rows):
    return lax.psum_scatter(
        term(jnp.int32(0), lax.axis_size("row") * local_rows),
        "row",
        scatter_dimension=0,
        tiled=True,
    )


def per_device(
    tokens,
    segment_ids,
    norm_gain,
    in_weight,
    conv_taps,
    out_weight,
    ffn_gain,
    gate_weight,
    up_weight,
    down_weight,
    out_grad,
):
    local_rows = tokens.shape[0]
    same_one = jnp.concatenate(
        [jnp.zeros((1,), jnp.float32), (segment_ids[1:] == segment_ids[:-1]).astype(jnp.float32)]
    )[:, None]
    same_two = jnp.concatenate(
        [jnp.zeros((2,), jnp.float32), (segment_ids[2:] == segment_ids[:-2]).astype(jnp.float32)]
    )[:, None]
    in_flat = in_weight.reshape(in_weight.shape[0], -1)
    scale_one = lax.rsqrt(sum_rows(tokens * tokens) / D + epsilon)
    normed_one = (tokens * scale_one * norm_gain).astype(jnp.bfloat16)
    normed_one_all = gather_rows(normed_one)
    group_rows = normed_one_all.shape[0]
    mixer_in = reduce_cols(
        jnp.dot(normed_one_all, in_flat, preferred_element_type=jnp.float32).reshape(
            group_rows, 3, -1
        )
    )
    gate_in = mixer_in[:, 0]
    gate_out = mixer_in[:, 1]
    carried = mixer_in[:, 2]
    product = gate_in * carried
    conv_out = (
        conv_taps[2] * product
        + conv_taps[1] * shifted(product, 1) * same_one
        + conv_taps[0] * shifted(product, 2) * same_two
    )
    mixed = (gate_out * conv_out).astype(jnp.bfloat16)
    mixed_all = share_cols(mixed[:, None, :])[:, 0, :]

    def mixer_fwd(offset, length):
        return jnp.dot(mixed_all, out_weight, preferred_element_type=jnp.float32)

    hidden_mid = tokens + reduce_rows(mixer_fwd, local_rows)
    scale_two = lax.rsqrt(sum_rows(hidden_mid * hidden_mid) / D + epsilon)
    normed_two = (hidden_mid * scale_two * ffn_gain).astype(jnp.bfloat16)
    normed_two_all = gather_rows(normed_two)
    both_proj = reduce_cols(
        jnp.stack(
            [
                jnp.dot(normed_two_all, gate_weight, preferred_element_type=jnp.float32),
                jnp.dot(normed_two_all, up_weight, preferred_element_type=jnp.float32),
            ],
            axis=1,
        )
    )
    gate_proj = both_proj[:, 0]
    up_proj = both_proj[:, 1]
    sigmoid_gate = jax.nn.sigmoid(gate_proj)
    activated = (gate_proj * sigmoid_gate * up_proj).astype(jnp.bfloat16)
    activated_all = share_cols(activated[:, None, :])[:, 0, :]

    def ffn_fwd(offset, length):
        return jnp.dot(activated_all, down_weight, preferred_element_type=jnp.float32)

    block_out = hidden_mid + reduce_rows(ffn_fwd, local_rows)
    grad_ffn = out_grad.astype(jnp.bfloat16)
    grad_ffn_all = gather_rows(grad_ffn)
    grad_down = dot_rows(activated_all, grad_ffn_all)
    grad_act = reduce_cols(dot_cols(grad_ffn_all, down_weight)[:, None, :])[:, 0, :]
    grad_up = grad_act * gate_proj * sigmoid_gate
    grad_gate = grad_act * up_proj * sigmoid_gate * (1.0 + gate_proj * (1.0 - sigmoid_gate))
    grad_pair = jnp.stack([grad_gate, grad_up], axis=1).astype(jnp.bfloat16)
    grad_pair_all = share_cols(grad_pair)
    grad_gate_w = dot_rows(normed_two_all, grad_pair_all[:, 0])
    grad_up_w = dot_rows(normed_two_all, grad_pair_all[:, 1])

    def ffn_back(offset, length):
        return dot_cols(grad_pair_all[:, 0], gate_weight) + dot_cols(grad_pair_all[:, 1], up_weight)

    grad_normed_two = reduce_rows(ffn_back, local_rows)
    gain_two_grad = jnp.sum(grad_normed_two * hidden_mid * scale_two, axis=0)
    weighted_two = ffn_gain * grad_normed_two
    cube_two = scale_two * scale_two * scale_two
    grad_mid = (
        out_grad
        + scale_two * weighted_two
        - hidden_mid * cube_two * (sum_rows(weighted_two * hidden_mid) / D)
    )
    grad_mix = grad_mid.astype(jnp.bfloat16)
    grad_mix_all = gather_rows(grad_mix)
    grad_out_w = dot_rows(mixed_all, grad_mix_all)
    grad_mixed = reduce_cols(dot_cols(grad_mix_all, out_weight)[:, None, :])[:, 0, :]
    grad_conv = grad_mixed * gate_out
    grad_product = (
        conv_taps[2] * grad_conv
        + conv_taps[1] * lifted(grad_conv * same_one, 1)
        + conv_taps[0] * lifted(grad_conv * same_two, 2)
    )
    taps_grad = jnp.stack(
        [
            jnp.sum(grad_conv * shifted(product, 2) * same_two, axis=0),
            jnp.sum(grad_conv * shifted(product, 1) * same_one, axis=0),
            jnp.sum(grad_conv * product, axis=0),
        ]
    )
    grad_triple = jnp.stack(
        [grad_product * carried, grad_mixed * conv_out, grad_product * gate_in], axis=1
    ).astype(jnp.bfloat16)
    grad_triple_all = share_cols(grad_triple)
    flat_grad = grad_triple_all.reshape(group_rows, -1)
    grad_in_w = dot_rows(normed_one_all, flat_grad).reshape(in_weight.shape)

    def mixer_back(offset, length):
        return dot_cols(flat_grad, in_flat)

    grad_normed_one = reduce_rows(mixer_back, local_rows)
    gain_one_grad = jnp.sum(grad_normed_one * tokens * scale_one, axis=0)
    weighted_one = norm_gain * grad_normed_one
    cube_one = scale_one * scale_one * scale_one
    in_grad = (
        grad_mid
        + scale_one * weighted_one
        - tokens * cube_one * (sum_rows(weighted_one * tokens) / D)
    )
    summed = lax.psum((grad_in_w, taps_grad, grad_out_w, grad_gate_w, grad_up_w, grad_down), "dp")
    gain_sums = lax.psum((gain_one_grad, gain_two_grad), ("dp", "row"))
    return (
        block_out,
        in_grad,
        gain_sums[0],
        summed[0],
        summed[1],
        summed[2],
        gain_sums[1],
        summed[3],
        summed[4],
        summed[5],
    )


def solution(mesh):
    in_specs = (
        P(("dp", "row"), "col"),
        P("dp"),
        P("col"),
        P("col", None, "row"),
        P(None, ("row", "col")),
        P("row", "col"),
        P("col"),
        P("col", "row"),
        P("col", "row"),
        P("row", "col"),
        P(("dp", "row"), "col"),
    )
    out_specs = (
        P(("dp", "row"), "col"),
        P(("dp", "row"), "col"),
        P("col"),
        P("col", None, "row"),
        P(None, ("row", "col")),
        P("row", "col"),
        P("col"),
        P("col", "row"),
        P("col", "row"),
        P("row", "col"),
    )
    return jax.shard_map(
        per_device, mesh=mesh, in_specs=in_specs, out_specs=out_specs, check_vma=False
    )
```

profile of v0, /device:TPU:0, one launch (start us, length us, event | category | flops | bytes accessed | tf_op | source)
XLA Modules:
  0.0 744.6 jit_solution(4233200987819264704)
XLA Ops:
  7.3 1.5 copy.39
  8.9 11.4 %psum.84 = f32[128,1]{0,1:T(1,128)S(1)} all-reduce(f32[128,1]{0,1:T(1,128)S(1)} %bitcast.150), channel_id=1, replica_groups=mesh['dp'=4,'row'=2,'col'=4] {'col'}, use_global_device_ids=true, to_apply=%region_1.0 | all-reduce | flops 128 | bytes 1024 | tf_op jit(solution)/shard_map/psum | solution.py:33
  21.4 1.9 all_gather.24
  23.9 1.5 fusion.17
  25.8 30.3 %reduce-scatter.7.cloned.1.call-done = f32[256,3,128]{2,0,1:T(8,128)} async-done(((f32[256,3,512]{2,0,1:T(8,128)}), f32[256,3,128]{2,0,1:T(8,128)}) %reduce-scatter.7.cloned.1.call-update) | async-done | bytes 393232 | tf_op jit(solution)/shard_map/reduce_scatter | solution.py:41
  56.1 1.0 fusion.22
  57.1 0.7 copy-done.11
  57.8 1.8 multiply_convert_fusion.6
  59.6 9.0 %all-gather = bf16[256,512]{1,0:T(8,128)(2,1)S(1)} all-gather(bf16[256,128]{1,0:T(8,128)(2,1)S(1)} %get-tuple-element.33), channel_id=2, replica_groups=mesh['dp'=4,'row'=2,'col'=4] {'col'}, dimensions={1}, use_global_device_ids=true | all-gather | bytes 327680 | tf_op jit(solution)/shard_map/all_gather | solution.py:45
  68.6 0.7 copy-done.14
  69.4 0.9 fusion.32
  70.4 1.9 all_gather.28
  72.3 0.7 copy-done.22
  73.0 1.8 convolution_bitcast_fusion
  74.8 3.9 copy.43
  78.7 1.1 multiply_reduce_fusion.7
  79.8 9.5 %psum.85 = f32[128,1]{0,1:T(1,128)S(1)} all-reduce(f32[128,1]{0,1:T(1,128)S(1)} %bitcast.147), channel_id=1, replica_groups=mesh['dp'=4,'row'=2,'col'=4] {'col'}, use_global_device_ids=true, to_apply=%region_5.0 | all-reduce | flops 128 | bytes 1024 | tf_op jit(solution)/shard_map/psum | solution.py:33
  89.9 1.9 all_gather.26
  92.5 0.7 copy-done.2
  93.6 2.5 pad_maximum_fusion
  96.1 8.1 %copy.40 = f32[256,2,2304]{0,1,2:T(2,128)} copy(f32[256,2,2304]{2,0,1:T(8,128)} %pad_maximum_fusion) | data formatting | bytes 9437184 | tf_op jit(solution)/shard_map/stack | solution.py:107
  106.1 148.5 %all-reduce.13.cloned.1.call-done = (f32[256,2,2304]{0,1,2:T(2,128)}, f32[256,1,2304]{0,1,2:T(1,128)}) async-done(((f32[256,2,2304]{0,1,2:T(2,128)}, f32[256,1,2304]{0,1,2:T(1,128)}), (f32[256,2,2304]{0,1,2:T(2,128)}, f32[256,1,2304]{0,1,2:T(1,128)})) %all-reduce.13.cloned.1.call-update) | async-done | bytes 7077904
  254.7 1.5 constant_dynamic-slice_fusion.1
  256.1 2.7 constant_dynamic-slice_fusion
  258.8 1.1 multiply_convert_fusion.1
  259.9 1.4 copy.46
  262.0 37.0 %all-gather.6.cloned.1.call-done = bf16[256,2,2304]{0,1,2:T(2,128)(2,1)} async-done(((bf16[256,2,576]{0,1,2:T(2,128)(2,1)}), bf16[256,2,2304]{0,1,2:T(2,128)(2,1)}) %all-gather.6.cloned.1.call-update) | async-done | bytes 2359312 | tf_op jit(solution)/shard_map/all_gather | solution.py:45
  299.0 7.9 %fusion.31 = (bf16[256,1,2304]{0,1,2:T(2,128)(2,1)}, bf16[256,1,2304]{0,1,2:T(2,128)(2,1)}) fusion(bf16[256,2,2304]{0,1,2:T(2,128)(2,1)} %all-gather.6.cloned.1.call-done), kind=kLoop, calls=%fused_computation.83 | loop fusion | bytes 4718592 | tf_op jit(solution)/shard_map/slice | solution.py:137
  306.9 5.0 copy.56
  311.9 5.0 copy.55
  317.4 0.8 copy-done.3
  318.2 1.2 fusion.12
  319.4 9.4 %all-gather.4.cloned.1.call-done = bf16[256,1,2304]{0,2,1:T(8,128)(2,1)} async-done(((bf16[256,1,576]{0,2,1:T(8,128)(2,1)}), bf16[256,1,2304]{0,2,1:T(8,128)(2,1)}) %all-gather.4.cloned.1.call-update) | async-done | bytes 1179664 | tf_op jit(solution)/shard_map/all_gather | solution.py:45
  328.9 2.5 fusion.10
  331.4 7.9 %reduce-scatter.13.cloned.1.call-done = f32[128,256]{1,0:T(8,128)} async-done(((f32[256,256]{1,0:T(8,128)}), f32[128,256]{1,0:T(8,128)}) %reduce-scatter.13.cloned.1.call-update) | async-done | bytes 131088 | tf_op jit(solution)/shard_map/reduce_scatter | solution.py:49
  339.3 1.7 multiply_reduce_fusion
  341.0 10.6 %psum.86 = f32[128,1]{0,1:T(1,128)} all-reduce(f32[128,1]{0,1:T(1,128)} %bitcast.148), channel_id=1, replica_groups=mesh['dp'=4,'row'=2,'col'=4] {'col'}, use_global_device_ids=true, to_apply=%region_11.0 | all-reduce | flops 128 | bytes 1024 | tf_op jit(solution)/shard_map/psum | solution.py:33
  351.6 1.2 multiply_bitcast_fusion.1
  352.8 1.9 fusion.30
  354.7 1.9 all_gather.30
  356.6 0.7 copy-done.23
  357.2 2.0 convolution_bitcast_fusion.3
  360.6 2.8 fusion.8
  363.4 1.9 fusion.4
  365.3 1.9 fusion
  367.3 16.6 %reduce-scatter.15.cloned.1.call-done = f32[256,1,128]{2,0,1:T(8,128)} async-done(((f32[256,1,512]{2,0,1:T(8,128)}), f32[256,1,128]{2,0,1:T(8,128)}) %reduce-scatter.15.cloned.1.call-update) | async-done | bytes 131088 | tf_op jit(solution)/shard_map/reduce_scatter | solution.py:41
  383.9 1.1 multiply_reduce_fusion.3
  385.3 11.5 %all_gather.31 = bf16[256,3,512]{2,0,1:T(8,128)(2,1)S(1)} all-gather(bf16[256,3,128]{2,0,1:T(8,128)(2,1)S(1)} %pad_maximum_fusion.2), channel_id=1, replica_groups=mesh['dp'=4,'row'=2,'col'=4] {'col'}, dimensions={2}, use_global_device_ids=true | all-gather | bytes 983040 | tf_op jit(solution)/shard_map/all_gather | solution.py:45
  396.8 1.1 convolution_bitcast_fusion.4
  398.0 1.1 fusion.33
  399.4 1.6 fusion.15
  401.0 12.4 %psum.90 = f32[3,128]{1,0:T(4,128)} all-reduce(f32[3,128]{1,0:T(4,128)S(1)} %pad_maximum_fusion.3), channel_id=1, replica_groups=mesh['dp'=4,'row'=2,'col'=4] {'dp'}, use_global_device_ids=true, to_apply=%region_22.0 | all-reduce | flops 384 | bytes 3072 | tf_op jit(solution)/shard_map/psum | solution.py:184
  413.4 1.0 multiply_reduce_fusion.4
  414.4 8.9 %psum.87 = f32[128,1]{0,1:T(1,128)S(1)} all-reduce(f32[128,1]{0,1:T(1,128)S(1)} %bitcast.149), channel_id=1, replica_groups=mesh['dp'=4,'row'=2,'col'=4] {'col'}, use_global_device_ids=true, to_apply=%region_15.0 | all-reduce | flops 128 | bytes 1024 | tf_op jit(solution)/shard_map/psum | solution.py:33
  423.4 14.9 %all-reduce.7 = (f32[256]{0:T(256)}, f32[256]{0:T(256)}) all-reduce(f32[256]{0:T(256)S(1)} %get-tuple-element.12, f32[256]{0:T(256)S(1)} %copy-done.42), channel_id=1, replica_groups=mesh['dp'=4,'row'=2,'col'=4] {'dp','row'}, use_global_device_ids=true, to_apply=%region_17.0 | all-reduce | flops 512 | bytes 4096 | tf_op jit(solution)/shard_map/psum | solution.py:185
  438.3 1.7 multiply_subtract_fusion
  440.0 287.7 %all-reduce.15.cloned.1.call-done = (f32[256,3,512]{2,0,1:T(8,128)}, f32[512,256]{1,0:T(8,128)}, f32[256,2304]{1,0:T(8,128)}, f32[256,2304]{1,0:T(8,128)}, f32[2304,256]{1,0:T(8,128)}) async-done(((f32[256,3,512]{2,0,1:T(8,128)}, f32[512,256]{1,0:T(8,128)}, f32[256,2304]{1,0:T(8,128)}, f32[256,2304]{1,0:T(8,128)}, f32[2304,256]{1,0:T(8,128)}), (f32[256,3,512]{2,0,1:T(8,128)}, f32[512,256]{1,0:T(8,128)}, ...) | async-done | bytes 9175056 | tf_op jit(solution)/shard_map/psum | solution.py:184
  727.7 2.8 copy.71
  730.5 0.8 copy.72
  731.3 1.4 copy.73
  732.7 1.1 copy-done.17
  733.9 1.4 copy.74
  735.3 1.1 copy-done.16
  736.4 1.4 copy.75
  (136 shorter events, 8.6 us)
Async XLA Ops:
  7.2 84.7 %copy-start = (bf16[256,2304]{1,0:T(8,128)(2,1)S(1)}, bf16[256,2304]{1,0:T(8,128)(2,1)}, u32[]{:S(2)}) copy-start(bf16[256,2304]{1,0:T(8,128)(2,1)} %param.19) | copy-start | bytes 3538948
  7.2 1.6 copy-start.9
  7.2 13.7 %copy-start.32 = (f32[256]{0:T(256)S(1)}, f32[256]{0:T(256)}, u32[]{:S(2)}) copy-start(f32[256]{0:T(256)} %param.13) | copy-start | bytes 3076
  7.2 48.9 %reduce-scatter.7.cloned.1.call-start = ((), (), s32[]{:S(2)}) async-start(), calls=%async_computation.6 | async-start | bytes 1966080 | tf_op jit(solution)/shard_map/reduce_scatter | solution.py:41
  20.9 0.5 copy-start.33
  23.3 0.7 copy-start.20
  23.9 1.6 copy-start.30
  23.9 1.9 copy-start.45
  25.5 43.9 %copy-start.25 = (bf16[512,256]{1,0:T(8,128)(2,1)S(1)}, bf16[512,256]{1,0:T(8,128)(2,1)}, u32[]{:S(2)}) copy-start(bf16[512,256]{1,0:T(8,128)(2,1)} %param.16) | copy-start | bytes 786436
  25.5 44.9 %copy-start.29 = (f32[128,256]{1,0:T(8,128)S(1)}, f32[128,256]{1,0:T(8,128)}, u32[]{:S(2)}) copy-start(f32[128,256]{1,0:T(8,128)} %param.21) | copy-start | bytes 393220
  25.5 53.2 %reduce-scatter.9.cloned.1.call-start = ((), (), s32[]{:S(2)}) async-start(), calls=%async_computation.7 | async-start | bytes 393216 | tf_op jit(solution)/shard_map/reduce_scatter | solution.py:49
  25.8 44.6 %copy-start.38 = (f32[128]{0:T(128)}, f32[128]{0:T(128)S(1)}, u32[]{:S(2)}) copy-start(f32[128]{0:T(128)S(1)} %get-tuple-element.45) | copy-start | bytes 1540
  25.8 44.6 %copy-start.40 = (f32[128]{0:T(128)}, f32[128]{0:T(128)S(1)}, u32[]{:S(2)}) copy-start(f32[128]{0:T(128)S(1)} %get-tuple-element.46) | copy-start | bytes 1540
  25.8 46.5 %copy-start.36 = (f32[128]{0:T(128)}, f32[128]{0:T(128)S(1)}, u32[]{:S(2)}) copy-start(f32[128]{0:T(128)S(1)} %get-tuple-element.44) | copy-start | bytes 1540
  57.1 0.7 copy-start.11
  68.6 0.7 copy-start.14
  70.3 184.3 %all-reduce.13.cloned.1.call-start = ((), (), s32[]{:S(2)}) async-start(), calls=%async_computation.14 | async-start | bytes 14155776
  72.3 0.7 copy-start.22
  74.7 15.1 %copy-start.31 = (f32[256]{0:T(256)S(1)}, f32[256]{0:T(256)}, u32[]{:S(2)}) copy-start(f32[256]{0:T(256)} %param.17) | copy-start | bytes 3076
  79.8 12.6 %copy-start.19 = (f32[128,256]{1,0:T(8,128)}, f32[128,256]{1,0:T(8,128)S(1)}, u32[]{:S(2)}) copy-start(f32[128,256]{1,0:T(8,128)S(1)} %get-tuple-element.32) | copy-start | bytes 393220
  89.8 2.5 copy-start.35
  91.8 0.7 copy-start.7
  91.8 1.3 copy-start.2
  104.2 0.7 copy-start.47
  104.3 194.7 %all-gather.6.cloned.1.call-start = ((), (), s32[]{:S(2)}) async-start(), calls=%async_computation.10 | async-start | bytes 2949120 | tf_op jit(solution)/shard_map/all_gather | solution.py:45
  261.4 67.5 %all-gather.4.cloned.1.call-start = ((), (), s32[]{:S(2)}) async-start(), calls=%async_computation.8 | async-start | bytes 1474560 | tf_op jit(solution)/shard_map/all_gather | solution.py:45
  261.9 77.3 %reduce-scatter.13.cloned.1.call-start = ((), (), s32[]{:S(2)}) async-start(), calls=%async_computation.11 | async-start | bytes 393216 | tf_op jit(solution)/shard_map/reduce_scatter | solution.py:49
  316.9 1.3 copy-start.3
  318.2 10.7 %copy-start.4 = (bf16[2304,256]{1,0:T(8,128)(2,1)S(1)}, bf16[2304,256]{1,0:T(8,128)(2,1)}, u32[]{:S(2)}) copy-start(bf16[2304,256]{1,0:T(8,128)(2,1)} %param.20) | copy-start | bytes 3538948
  319.4 33.4 %reduce-scatter.11.cloned.1.call-start = ((), (), s32[]{:S(2)}) async-start(), calls=%async_computation.9 | async-start | bytes 393216 | tf_op jit(solution)/shard_map/reduce_scatter | solution.py:49
  331.4 29.2 %copy-start.5 = (bf16[256,1,2304]{0,2,1:T(8,128)(2,1)S(1)}, bf16[256,1,2304]{0,2,1:T(8,128)(2,1)}, u32[]{:S(2)}) copy-start(bf16[256,1,2304]{0,2,1:T(8,128)(2,1)} %all-gather.4.cloned.1.call-done) | copy-start | bytes 3538948
  331.4 52.5 %reduce-scatter.15.cloned.1.call-start = ((), (), s32[]{:S(2)}) async-start(), calls=%async_computation.12 | async-start | bytes 655360 | tf_op jit(solution)/shard_map/reduce_scatter | solution.py:41
  356.6 0.7 copy-start.23
  359.3 54.1 %reduce-scatter.17.cloned.1.call-start = ((), (), s32[]{:S(2)}) async-start(), calls=%async_computation.13 | async-start | bytes 393216 | tf_op jit(solution)/shard_map/reduce_scatter | solution.py:49
  360.6 2.8 copy-start.8
  365.3 18.6 %copy-start.6 = (f32[256,3,128]{2,0,1:T(8,128)S(1)}, f32[256,3,128]{2,0,1:T(8,128)}, u32[]{:S(2)}) copy-start(f32[256,3,128]{2,0,1:T(8,128)} %reduce-scatter.7.cloned.1.call-done) | copy-start | bytes 1179652
  365.3 18.6 %copy-start.12 = (f32[256,128]{1,0:T(8,128)S(1)}, f32[256,128]{1,0:T(8,128)}, u32[]{:S(2)}) copy-start(f32[256,128]{1,0:T(8,128)} %copy-done.11) | copy-start | bytes 393220
  365.3 18.6 %copy-start.27 = (f32[256,128]{1,0:T(8,128)S(1)}, f32[256,128]{1,0:T(8,128)}, u32[]{:S(2)}) copy-start(f32[256,128]{1,0:T(8,128)} %get-tuple-element.34) | copy-start | bytes 393220
  365.3 19.6 %copy-start.44 = (f32[254]{0:T(256)S(1)}, f32[254]{0:T(256)}, u32[]{:S(2)}) copy-start(f32[254]{0:T(256)} %slice.89) | copy-start | bytes 3052
  365.3 19.7 %copy-start.43 = (f32[255]{0:T(256)S(1)}, f32[255]{0:T(256)}, u32[]{:S(2)}) copy-start(f32[255]{0:T(256)} %slice.87) | copy-start | bytes 3064
  367.3 17.9 %copy-start.37 = (f32[128]{0:T(128)S(1)}, f32[128]{0:T(128)}, u32[]{:S(2)}) copy-start(f32[128]{0:T(128)} %copy-done.36) | copy-start | bytes 1540
  367.3 17.9 %copy-start.39 = (f32[128]{0:T(128)S(1)}, f32[128]{0:T(128)}, u32[]{:S(2)}) copy-start(f32[128]{0:T(128)} %copy-done.38) | copy-start | bytes 1540
  367.3 17.9 %copy-start.41 = (f32[128]{0:T(128)S(1)}, f32[128]{0:T(128)}, u32[]{:S(2)}) copy-start(f32[128]{0:T(128)} %copy-done.40) | copy-start | bytes 1540
  384.9 11.9 %copy-start.13 = (bf16[256,3,512]{2,0,1:T(8,128)(2,1)S(1)}, bf16[256,3,512]{2,0,1:T(8,128)(2,1)}, u32[]{:S(2)}) copy-start(bf16[256,3,512]{2,0,1:T(8,128)(2,1)} %param.14) | copy-start | bytes 2359300
  385.3 12.7 %copy-start.15 = (bf16[256,512]{1,0:T(8,128)(2,1)S(1)}, bf16[256,512]{1,0:T(8,128)(2,1)}, u32[]{:S(2)}) copy-start(bf16[256,512]{1,0:T(8,128)(2,1)} %copy-done.14) | copy-start | bytes 786436
  385.3 12.7 %copy-start.24 = (bf16[256,256]{1,0:T(8,128)(2,1)S(1)}, bf16[256,256]{1,0:T(8,128)(2,1)}, u32[]{:S(2)}) copy-start(bf16[256,256]{1,0:T(8,128)(2,1)} %copy-done.23) | copy-start | bytes 393220
  397.9 1.4 copy-start.21
  397.9 329.8 %all-reduce.15.cloned.1.call-start = ((), (), s32[]{:S(2)}) async-start(), calls=%async_computation.15 | async-start | bytes 18350080 | tf_op jit(solution)/shard_map/psum | solution.py:184
  400.9 12.5 %copy-start.10 = (f32[128,256]{1,0:T(8,128)S(1)}, f32[128,256]{1,0:T(8,128)}, u32[]{:S(2)}) copy-start(f32[128,256]{1,0:T(8,128)} %param.11) | copy-start | bytes 393220
  400.9 12.5 %copy-start.34 = (f32[128]{0:T(128)S(1)}, f32[128]{0:T(128)}, u32[]{:S(2)}) copy-start(f32[128]{0:T(128)} %copy-done.33) | copy-start | bytes 1540
  400.9 22.4 %copy-start.42 = (f32[256]{0:T(256)S(1)}, f32[256]{0:T(256)}, u32[]{:S(2)}) copy-start(f32[256]{0:T(256)} %get-tuple-element.10) | copy-start | bytes 3076
  400.9 37.4 %copy-start.28 = (f32[128,256]{1,0:T(8,128)S(1)}, f32[128,256]{1,0:T(8,128)}, u32[]{:S(2)}) copy-start(f32[128,256]{1,0:T(8,128)} %get-tuple-element.30) | copy-start | bytes 393220
  400.9 37.4 %copy-start.46 = (f32[128]{0:T(128)S(1)}, f32[128]{0:T(128)}, u32[]{:S(2)}) copy-start(f32[128]{0:T(128)} %get-tuple-element.47) | copy-start | bytes 1540
  727.7 2.8 copy-start.26
  727.7 3.6 copy-start.18
  731.3 2.5 copy-start.17
  733.9 2.5 copy-start.16
  733.9 3.9 copy-start.1
Sparse Core Ops, SparseCore 0:
  25.6 30.4 reduce-scatter.6
  70.4 7.7 reduce-scatter.8
  104.4 150.2 all-reduce.12
  261.5 37.4 all-gather.5
  301.3 27.5 all-gather.3
  331.5 7.7 reduce-scatter.12
  342.1 8.8 reduce-scatter.10
  359.4 24.4 reduce-scatter.14
  398.1 7.7 reduce-scatter.16
  409.9 317.7 all-reduce.14
where the time goes:
time: 746 us; the launch traced here: 745 us
  waiting for transfers between devices  538 us (72%)
  blocking collectives  95.9 us (13%)
  local copies, waits for them, and re-layouts  55.2 us (7%)
  matrix products  21.8 us (3%)
  other arithmetic  17.9 us (2%)
  between operations  15.3 us (2%)
    psum x1, waiting for transfers between devices, per_device(): lax.psum((grad_in_w, taps_grad, grad_out_w, grad_gate_w, grad_up_w, grad_...  288 us
    unnamed x11, waiting for transfers between devices  149 us
    reduce_scatter x2, waiting for transfers between devices, reduce_cols(): lax.psum_scatter(partial_value, 'col', scatter_dimension=2, tiled=True)  46.9 us
    all_gather x2, waiting for transfers between devices, share_cols(): return lax.all_gather(shard_part, 'col', axis=2, tiled=True)  46.4 us
    psum x4, blocking collectives, sum_rows(): return lax.psum(jnp.sum(entries, axis=1, keepdims=True), 'col')  40.5 us
    unnamed x106, local copies, waits for them, and re-layouts  29.6 us
    all_gather x2, blocking collectives, share_cols(): return lax.all_gather(shard_part, 'col', axis=2, tiled=True)  20.5 us
    psum x1, blocking collectives, per_device(): gain_sums = lax.psum((gain_one_grad, gain_two_grad), ('dp', 'row'))  14.9 us
  transfers between devices with their start and end apart: 10, of which 7 were waited for; matrix products, arithmetic and copies ran while one was open for 6% of the time, Pallas kernels for 0%

commit v1 on v0

--- a/solution.py
+++ b/solution.py
@@ -30,7 +30,7 @@
 
 
 def sum_rows(entries):
-    return lax.psum(jnp.sum(entries, axis=1, keepdims=True), "col")
+    return jnp.sum(lax.all_gather(jnp.sum(entries, axis=1, keepdims=True), "col"), axis=0)
 
 
 def gather_rows(shard_part):

time: 746 us -> 744 us (level)
  blocking collectives: 95.9 us -> 87.7 us
    psum x4 -> x0, blocking collectives: 40.5 us -> none  [sum_rows(): return lax.psum(jnp.sum(entries, axis=1, keepdims=True), 'col')]
    all_gather x0 -> x4, blocking collectives: none -> 32.2 us  [sum_rows(): lax.all_gather(jnp.sum(entries, axis=1, keepdims=True), 'col')]
where the time goes in v1:
time: 744 us; the launch traced here: 742 us
  waiting for transfers between devices  543 us (73%)
  blocking collectives  87.7 us (12%)
  local copies, waits for them, and re-layouts  55.2 us (7%)
  matrix products  21.8 us (3%)
  other arithmetic  19.2 us (3%)
  between operations  15.3 us (2%)
    psum x1, waiting for transfers between devices, per_device(): lax.psum((grad_in_w, taps_grad, grad_out_w, grad_gate_w, grad_up_w, grad_...  290 us
    unnamed x11, waiting for transfers between devices  150 us
    reduce_scatter x2, waiting for transfers between devices, reduce_cols(): lax.psum_scatter(partial_value, 'col', scatter_dimension=2, tiled=True)  48.9 us
    all_gather x2, waiting for transfers between devices, share_cols(): return lax.all_gather(shard_part, 'col', axis=2, tiled=True)  46.4 us
    all_gather x4, blocking collectives, sum_rows(): lax.all_gather(jnp.sum(entries, axis=1, keepdims=True), 'col')  32.2 us
    unnamed x106, local copies, waits for them, and re-layouts  29.6 us
    all_gather x2, blocking collectives, share_cols(): return lax.all_gather(shard_part, 'col', axis=2, tiled=True)  20.5 us
    psum x1, blocking collectives, per_device(): gain_sums = lax.psum((gain_one_grad, gain_two_grad), ('dp', 'row'))  15.1 us
  transfers between devices with their start and end apart: 10, of which 7 were waited for; matrix products, arithmetic and copies ran while one was open for 6% of the time, Pallas kernels for 0%

profile of v1, /device:TPU:0, one launch (start us, length us, event | category | flops | bytes accessed | tf_op | source)
XLA Modules:
  0.0 742.5 jit_solution(18262495066495899412)
XLA Ops:
  7.3 1.5 copy.39
  8.9 9.4 %all-gather.5 = f32[4,1,128]{2,1,0:T(1,128)S(1)} all-gather(f32[1,1,128]{2,1,0:T(1,128)S(1)} %bitcast.138), channel_id=2, replica_groups=mesh['dp'=4,'row'=2,'col'=4] {'col'}, dimensions={0}, use_global_device_ids=true | all-gather | bytes 2560 | tf_op jit(solution)/shard_map/all_gather | solution.py:33
  19.4 1.9 all_gather.37
  22.0 1.5 fusion.17
  23.9 31.3 %reduce-scatter.7.cloned.1.call-done = f32[256,3,128]{2,0,1:T(8,128)} async-done(((f32[256,3,512]{2,0,1:T(8,128)}), f32[256,3,128]{2,0,1:T(8,128)}) %reduce-scatter.7.cloned.1.call-update) | async-done | bytes 393232 | tf_op jit(solution)/shard_map/reduce_scatter | solution.py:41
  55.2 1.0 fusion.22
  56.2 0.7 copy-done.11
  56.8 1.8 multiply_convert_fusion.6
  58.6 9.0 %all-gather.1 = bf16[256,512]{1,0:T(8,128)(2,1)S(1)} all-gather(bf16[256,128]{1,0:T(8,128)(2,1)S(1)} %get-tuple-element.33), channel_id=3, replica_groups=mesh['dp'=4,'row'=2,'col'=4] {'col'}, dimensions={1}, use_global_device_ids=true | all-gather | bytes 327680 | tf_op jit(solution)/shard_map/all_gather | solution.py:45
  67.6 0.7 copy-done.14
  68.4 0.9 fusion.28
  69.4 1.9 all_gather.42
  72.0 1.8 convolution_bitcast_fusion
  73.8 3.9 copy.43
  77.7 1.1 multiply_reduce_fusion.7
  78.8 7.6 %all-gather.6 = f32[4,1,128]{2,1,0:T(1,128)S(1)} all-gather(f32[1,1,128]{2,1,0:T(1,128)S(1)} %bitcast.135), channel_id=4, replica_groups=mesh['dp'=4,'row'=2,'col'=4] {'col'}, dimensions={0}, use_global_device_ids=true | all-gather | bytes 2560 | tf_op jit(solution)/shard_map/all_gather | solution.py:33
  87.0 1.9 all_gather.40
  89.6 0.7 copy-done.2
  90.7 2.5 pad_maximum_fusion
  93.2 8.1 %copy.40 = f32[256,2,2304]{0,1,2:T(2,128)} copy(f32[256,2,2304]{2,0,1:T(8,128)} %pad_maximum_fusion) | data formatting | bytes 9437184 | tf_op jit(solution)/shard_map/stack | solution.py:107
  103.2 149.4 %all-reduce.13.cloned.1.call-done = (f32[256,2,2304]{0,1,2:T(2,128)}, f32[256,1,2304]{0,1,2:T(1,128)}) async-done(((f32[256,2,2304]{0,1,2:T(2,128)}, f32[256,1,2304]{0,1,2:T(1,128)}), (f32[256,2,2304]{0,1,2:T(2,128)}, f32[256,1,2304]{0,1,2:T(1,128)})) %all-reduce.13.cloned.1.call-update) | async-done | bytes 7077904
  252.6 1.5 constant_dynamic-slice_fusion.1
  254.1 2.7 constant_dynamic-slice_fusion
  256.7 1.1 multiply_convert_fusion.1
  257.9 1.4 copy.46
  260.0 37.0 %all-gather.14.cloned.1.call-done = bf16[256,2,2304]{0,1,2:T(2,128)(2,1)} async-done(((bf16[256,2,576]{0,1,2:T(2,128)(2,1)}), bf16[256,2,2304]{0,1,2:T(2,128)(2,1)}) %all-gather.14.cloned.1.call-update) | async-done | bytes 2359312 | tf_op jit(solution)/shard_map/all_gather | solution.py:45
  297.0 7.9 %fusion.27 = (bf16[256,1,2304]{0,1,2:T(2,128)(2,1)}, bf16[256,1,2304]{0,1,2:T(2,128)(2,1)}) fusion(bf16[256,2,2304]{0,1,2:T(2,128)(2,1)} %all-gather.14.cloned.1.call-done), kind=kLoop, calls=%fused_computation.79 | loop fusion | bytes 4718592 | tf_op jit(solution)/shard_map/slice | solution.py:137
  304.9 5.0 copy.56
  309.9 5.0 copy.55
  315.4 0.8 copy-done.3
  316.1 1.2 fusion.12
  317.4 9.4 %all-gather.12.cloned.1.call-done = bf16[256,1,2304]{0,2,1:T(8,128)(2,1)} async-done(((bf16[256,1,576]{0,2,1:T(8,128)(2,1)}), bf16[256,1,2304]{0,2,1:T(8,128)(2,1)}) %all-gather.12.cloned.1.call-update) | async-done | bytes 1179664 | tf_op jit(solution)/shard_map/all_gather | solution.py:45
  326.8 2.5 fusion.10
  329.4 7.9 %reduce-scatter.13.cloned.1.call-done = f32[128,256]{1,0:T(8,128)} async-done(((f32[256,256]{1,0:T(8,128)}), f32[128,256]{1,0:T(8,128)}) %reduce-scatter.13.cloned.1.call-update) | async-done | bytes 131088 | tf_op jit(solution)/shard_map/reduce_scatter | solution.py:49
  337.3 1.7 multiply_reduce_fusion
  338.9 8.4 %all-gather.7 = f32[4,1,128]{2,1,0:T(1,128)} all-gather(f32[1,1,128]{2,1,0:T(1,128)S(1)} %bitcast.136), channel_id=5, replica_groups=mesh['dp'=4,'row'=2,'col'=4] {'col'}, dimensions={0}, use_global_device_ids=true | all-gather | bytes 2560 | tf_op jit(solution)/shard_map/all_gather | solution.py:33
  347.4 1.2 reduce.6
  348.6 1.2 broadcast_multiply_fusion.1
  349.7 1.9 fusion.26
  351.6 1.9 all_gather.45
  353.5 0.7 copy-done.23
  354.2 2.0 convolution_bitcast_fusion.3
  357.5 2.8 fusion.8
  360.3 1.9 fusion.4
  362.3 1.9 fusion
  364.2 17.6 %reduce-scatter.15.cloned.1.call-done = f32[256,1,128]{2,0,1:T(8,128)} async-done(((f32[256,1,512]{2,0,1:T(8,128)}), f32[256,1,128]{2,0,1:T(8,128)}) %reduce-scatter.15.cloned.1.call-update) | async-done | bytes 131088 | tf_op jit(solution)/shard_map/reduce_scatter | solution.py:41
  381.8 1.1 multiply_reduce_fusion.3
  383.3 11.5 %all_gather.46 = bf16[256,3,512]{2,0,1:T(8,128)(2,1)S(1)} all-gather(bf16[256,3,128]{2,0,1:T(8,128)(2,1)S(1)} %pad_maximum_fusion.2), channel_id=1, replica_groups=mesh['dp'=4,'row'=2,'col'=4] {'col'}, dimensions={2}, use_global_device_ids=true | all-gather | bytes 983040 | tf_op jit(solution)/shard_map/all_gather | solution.py:45
  394.8 1.1 convolution_bitcast_fusion.4
  396.0 1.1 fusion.29
  397.3 1.6 fusion.15
  398.9 12.4 %psum.58 = f32[3,128]{1,0:T(4,128)} all-reduce(f32[3,128]{1,0:T(4,128)S(1)} %pad_maximum_fusion.3), channel_id=1, replica_groups=mesh['dp'=4,'row'=2,'col'=4] {'dp'}, use_global_device_ids=true, to_apply=%region_22.0 | all-reduce | flops 384 | bytes 3072 | tf_op jit(solution)/shard_map/psum | solution.py:184
  411.4 1.0 multiply_reduce_fusion.4
  412.4 6.7 all-gather.8
  419.1 15.1 %all-reduce.7 = (f32[256]{0:T(256)}, f32[256]{0:T(256)}) all-reduce(f32[256]{0:T(256)S(1)} %get-tuple-element.12, f32[256]{0:T(256)S(1)} %copy-done.42), channel_id=1, replica_groups=mesh['dp'=4,'row'=2,'col'=4] {'dp','row'}, use_global_device_ids=true, to_apply=%region_17.0 | all-reduce | flops 512 | bytes 4096 | tf_op jit(solution)/shard_map/psum | solution.py:185
  434.2 1.7 multiply_subtract_fusion
  435.9 289.7 %all-reduce.15.cloned.1.call-done = (f32[256,3,512]{2,0,1:T(8,128)}, f32[512,256]{1,0:T(8,128)}, f32[256,2304]{1,0:T(8,128)}, f32[256,2304]{1,0:T(8,128)}, f32[2304,256]{1,0:T(8,128)}) async-done(((f32[256,3,512]{2,0,1:T(8,128)}, f32[512,256]{1,0:T(8,128)}, f32[256,2304]{1,0:T(8,128)}, f32[256,2304]{1,0:T(8,128)}, f32[2304,256]{1,0:T(8,128)}), (f32[256,3,512]{2,0,1:T(8,128)}, f32[512,256]{1,0:T(8,128)}, ...) | async-done | bytes 9175056 | tf_op jit(solution)/shard_map/psum | solution.py:184
  725.6 2.8 copy.71
  728.4 0.8 copy.72
  729.2 1.4 copy.73
  730.6 1.1 copy-done.17
  731.7 1.4 copy.74
  733.1 1.1 copy-done.16
  734.2 1.4 copy.75
  (140 shorter events, 9.3 us)
Async XLA Ops:
  7.2 81.8 %copy-start = (bf16[256,2304]{1,0:T(8,128)(2,1)S(1)}, bf16[256,2304]{1,0:T(8,128)(2,1)}, u32[]{:S(2)}) copy-start(bf16[256,2304]{1,0:T(8,128)(2,1)} %param.19) | copy-start | bytes 3538948
  7.2 1.6 copy-start.9
  7.2 11.7 %copy-start.32 = (f32[256]{0:T(256)S(1)}, f32[256]{0:T(256)}, u32[]{:S(2)}) copy-start(f32[256]{0:T(256)} %param.13) | copy-start | bytes 3076
  7.2 47.9 %reduce-scatter.7.cloned.1.call-start = ((), (), s32[]{:S(2)}) async-start(), calls=%async_computation.6 | async-start | bytes 1966080 | tf_op jit(solution)/shard_map/reduce_scatter | solution.py:41
  18.9 0.5 copy-start.33
  21.3 0.7 copy-start.20
  22.0 1.6 copy-start.30
  22.0 1.9 copy-start.45
  23.5 44.8 %copy-start.25 = (bf16[512,256]{1,0:T(8,128)(2,1)S(1)}, bf16[512,256]{1,0:T(8,128)(2,1)}, u32[]{:S(2)}) copy-start(bf16[512,256]{1,0:T(8,128)(2,1)} %param.16) | copy-start | bytes 786436
  23.6 45.8 %copy-start.29 = (f32[128,256]{1,0:T(8,128)S(1)}, f32[128,256]{1,0:T(8,128)}, u32[]{:S(2)}) copy-start(f32[128,256]{1,0:T(8,128)} %param.21) | copy-start | bytes 393220
  23.6 54.1 %reduce-scatter.9.cloned.1.call-start = ((), (), s32[]{:S(2)}) async-start(), calls=%async_computation.7 | async-start | bytes 393216 | tf_op jit(solution)/shard_map/reduce_scatter | solution.py:49
  23.9 45.5 %copy-start.38 = (f32[128]{0:T(128)}, f32[128]{0:T(128)S(1)}, u32[]{:S(2)}) copy-start(f32[128]{0:T(128)S(1)} %get-tuple-element.45) | copy-start | bytes 1540
  23.9 45.5 %copy-start.40 = (f32[128]{0:T(128)}, f32[128]{0:T(128)S(1)}, u32[]{:S(2)}) copy-start(f32[128]{0:T(128)S(1)} %get-tuple-element.46) | copy-start | bytes 1540
  23.9 47.4 %copy-start.36 = (f32[128]{0:T(128)}, f32[128]{0:T(128)S(1)}, u32[]{:S(2)}) copy-start(f32[128]{0:T(128)S(1)} %get-tuple-element.44) | copy-start | bytes 1540
  56.1 0.7 copy-start.11
  67.6 0.7 copy-start.14
  69.3 183.3 %all-reduce.13.cloned.1.call-start = ((), (), s32[]{:S(2)}) async-start(), calls=%async_computation.14 | async-start | bytes 14155776
  71.3 0.7 copy-start.22
  73.7 13.2 %copy-start.31 = (f32[256]{0:T(256)S(1)}, f32[256]{0:T(256)}, u32[]{:S(2)}) copy-start(f32[256]{0:T(256)} %param.17) | copy-start | bytes 3076
  78.8 10.7 %copy-start.19 = (f32[128,256]{1,0:T(8,128)}, f32[128,256]{1,0:T(8,128)S(1)}, u32[]{:S(2)}) copy-start(f32[128,256]{1,0:T(8,128)S(1)} %get-tuple-element.32) | copy-start | bytes 393220
  86.9 2.5 copy-start.35
  88.9 0.7 copy-start.7
  88.9 1.3 copy-start.2
  101.3 0.7 copy-start.47
  101.4 195.6 %all-gather.14.cloned.1.call-start = ((), (), s32[]{:S(2)}) async-start(), calls=%async_computation.10 | async-start | bytes 2949120 | tf_op jit(solution)/shard_map/all_gather | solution.py:45
  259.3 67.5 %all-gather.12.cloned.1.call-start = ((), (), s32[]{:S(2)}) async-start(), calls=%async_computation.8 | async-start | bytes 1474560 | tf_op jit(solution)/shard_map/all_gather | solution.py:45
  259.9 77.3 %reduce-scatter.13.cloned.1.call-start = ((), (), s32[]{:S(2)}) async-start(), calls=%async_computation.11 | async-start | bytes 393216 | tf_op jit(solution)/shard_map/reduce_scatter | solution.py:49
  314.9 1.3 copy-start.3
  316.1 10.7 %copy-start.4 = (bf16[2304,256]{1,0:T(8,128)(2,1)S(1)}, bf16[2304,256]{1,0:T(8,128)(2,1)}, u32[]{:S(2)}) copy-start(bf16[2304,256]{1,0:T(8,128)(2,1)} %param.20) | copy-start | bytes 3538948
  317.4 32.3 %reduce-scatter.11.cloned.1.call-start = ((), (), s32[]{:S(2)}) async-start(), calls=%async_computation.9 | async-start | bytes 393216 | tf_op jit(solution)/shard_map/reduce_scatter | solution.py:49
  329.3 28.2 %copy-start.5 = (bf16[256,1,2304]{0,2,1:T(8,128)(2,1)S(1)}, bf16[256,1,2304]{0,2,1:T(8,128)(2,1)}, u32[]{:S(2)}) copy-start(bf16[256,1,2304]{0,2,1:T(8,128)(2,1)} %all-gather.12.cloned.1.call-done) | copy-start | bytes 3538948
  329.4 52.5 %reduce-scatter.15.cloned.1.call-start = ((), (), s32[]{:S(2)}) async-start(), calls=%async_computation.12 | async-start | bytes 655360 | tf_op jit(solution)/shard_map/reduce_scatter | solution.py:41
  353.5 0.7 copy-start.23
  356.2 55.1 %reduce-scatter.17.cloned.1.call-start = ((), (), s32[]{:S(2)}) async-start(), calls=%async_computation.13 | async-start | bytes 393216 | tf_op jit(solution)/shard_map/reduce_scatter | solution.py:49
  357.5 2.8 copy-start.8
  362.3 19.6 %copy-start.6 = (f32[256,3,128]{2,0,1:T(8,128)S(1)}, f32[256,3,128]{2,0,1:T(8,128)}, u32[]{:S(2)}) copy-start(f32[256,3,128]{2,0,1:T(8,128)} %reduce-scatter.7.cloned.1.call-done) | copy-start | bytes 1179652
  362.3 19.6 %copy-start.12 = (f32[256,128]{1,0:T(8,128)S(1)}, f32[256,128]{1,0:T(8,128)}, u32[]{:S(2)}) copy-start(f32[256,128]{1,0:T(8,128)} %copy-done.11) | copy-start | bytes 393220
  362.3 19.6 %copy-start.27 = (f32[256,128]{1,0:T(8,128)S(1)}, f32[256,128]{1,0:T(8,128)}, u32[]{:S(2)}) copy-start(f32[256,128]{1,0:T(8,128)} %get-tuple-element.34) | copy-start | bytes 393220
  362.3 20.6 %copy-start.44 = (f32[254]{0:T(256)S(1)}, f32[254]{0:T(256)}, u32[]{:S(2)}) copy-start(f32[254]{0:T(256)} %slice.89) | copy-start | bytes 3052
  362.3 20.7 %copy-start.43 = (f32[255]{0:T(256)S(1)}, f32[255]{0:T(256)}, u32[]{:S(2)}) copy-start(f32[255]{0:T(256)} %slice.87) | copy-start | bytes 3064
  364.2 18.9 %copy-start.37 = (f32[128]{0:T(128)S(1)}, f32[128]{0:T(128)}, u32[]{:S(2)}) copy-start(f32[128]{0:T(128)} %copy-done.36) | copy-start | bytes 1540
  364.2 18.9 %copy-start.39 = (f32[128]{0:T(128)S(1)}, f32[128]{0:T(128)}, u32[]{:S(2)}) copy-start(f32[128]{0:T(128)} %copy-done.38) | copy-start | bytes 1540
  364.2 18.9 %copy-start.41 = (f32[128]{0:T(128)S(1)}, f32[128]{0:T(128)}, u32[]{:S(2)}) copy-start(f32[128]{0:T(128)} %copy-done.40) | copy-start | bytes 1540
  382.9 11.9 %copy-start.13 = (bf16[256,3,512]{2,0,1:T(8,128)(2,1)S(1)}, bf16[256,3,512]{2,0,1:T(8,128)(2,1)}, u32[]{:S(2)}) copy-start(bf16[256,3,512]{2,0,1:T(8,128)(2,1)} %param.14) | copy-start | bytes 2359300
  383.3 12.7 %copy-start.15 = (bf16[256,512]{1,0:T(8,128)(2,1)S(1)}, bf16[256,512]{1,0:T(8,128)(2,1)}, u32[]{:S(2)}) copy-start(bf16[256,512]{1,0:T(8,128)(2,1)} %copy-done.14) | copy-start | bytes 786436
  383.3 12.7 %copy-start.24 = (bf16[256,256]{1,0:T(8,128)(2,1)S(1)}, bf16[256,256]{1,0:T(8,128)(2,1)}, u32[]{:S(2)}) copy-start(bf16[256,256]{1,0:T(8,128)(2,1)} %copy-done.23) | copy-start | bytes 393220
  395.9 1.4 copy-start.21
  395.9 329.7 %all-reduce.15.cloned.1.call-start = ((), (), s32[]{:S(2)}) async-start(), calls=%async_computation.15 | async-start | bytes 18350080 | tf_op jit(solution)/shard_map/psum | solution.py:184
  398.9 12.5 %copy-start.10 = (f32[128,256]{1,0:T(8,128)S(1)}, f32[128,256]{1,0:T(8,128)}, u32[]{:S(2)}) copy-start(f32[128,256]{1,0:T(8,128)} %param.11) | copy-start | bytes 393220
  398.9 12.5 %copy-start.34 = (f32[128]{0:T(128)S(1)}, f32[128]{0:T(128)}, u32[]{:S(2)}) copy-start(f32[128]{0:T(128)} %copy-done.33) | copy-start | bytes 1540
  398.9 20.3 %copy-start.42 = (f32[256]{0:T(256)S(1)}, f32[256]{0:T(256)}, u32[]{:S(2)}) copy-start(f32[256]{0:T(256)} %get-tuple-element.10) | copy-start | bytes 3076
  398.9 35.4 %copy-start.28 = (f32[128,256]{1,0:T(8,128)S(1)}, f32[128,256]{1,0:T(8,128)}, u32[]{:S(2)}) copy-start(f32[128,256]{1,0:T(8,128)} %get-tuple-element.30) | copy-start | bytes 393220
  398.9 35.4 %copy-start.46 = (f32[128]{0:T(128)S(1)}, f32[128]{0:T(128)}, u32[]{:S(2)}) copy-start(f32[128]{0:T(128)} %get-tuple-element.47) | copy-start | bytes 1540
  725.6 2.8 copy-start.26
  725.6 3.6 copy-start.18
  729.2 2.5 copy-start.17
  731.7 2.5 copy-start.16
  731.7 3.9 copy-start.1
Sparse Core Ops, SparseCore 0:
  23.7 31.4 reduce-scatter.6
  69.4 7.7 reduce-scatter.8
  101.5 151.0 all-reduce.12
  259.4 37.4 all-gather.13
  299.2 27.5 all-gather.11
  329.5 7.7 reduce-scatter.12
  340.1 8.8 reduce-scatter.10
  356.3 25.4 reduce-scatter.14
  396.0 7.7 reduce-scatter.16
  407.9 317.6 all-reduce.14
